TPU v7x, 256 devices: a whole 4x4x8 slice. The times are simulated.
256 devices in a mesh: wide: 64 (over y, z, core), narrow: 4 (over x).
Axes of the slice: x: 4, y: 4, z: 8, core: 2. Of those that a mesh axis runs over, the one named last changes fastest.
Arguments:
- upper_panel: float32 [15360, 1024], P('wide', 'narrow'), may hold values from -0.1875 to 0.1875
- coupling: float32 [512, 512], P('wide'), may hold values from -0.25 to 0.25
- diag_inverse: float32 [2, 512, 512], replicated, as said below
- block_rhs: float32 [2, 512, 2048], P(None, 'wide'), may hold values from -6 to 6
- upper_rhs: float32 [15360, 2048], P('wide', 'narrow'), may hold values from -6 to 6
Outputs:
- solved: float32 [2, 512, 2048], P(None, 'wide', 'narrow')
- updated: float32 [15360, 2048], P('wide', 'narrow')
Inputs may be any that keep to these rules, and one draw needn't show every extreme that they name: Each diag_inverse[k] is upper triangular with a positive diagonal.
All inputs are finite; a program needn't handle non-finite values.
Results may differ from a plain program's by a relative error of at most 0.000088.
Values sent between devices are 32-bit elements; how exact they have to be, the bound alone decides.
No kernel may reach another device: no remote copies, remote signals or barrier semaphores. Data moves between devices by JAX's collectives and lax.ppermute only.
A program may use at most 64 MiB of HBM per device.

v0:
```python
import jax
import jax.numpy as jnp
from jax import lax
from jax.sharding import PartitionSpec as P


def product(left, right):
    return jnp.dot(left, right, precision=lax.Precision.HIGHEST, preferred_element_type=jnp.float32)


def local(upper_panel, coupling, diag_inverse, block_rhs, upper_rhs):
    wide_index = lax.axis_index("wide")
    narrow_index = lax.axis_index("narrow")
    block_rows = block_rhs.shape[1]
    own_targets = upper_rhs.shape[1]
    panel_width = upper_panel.shape[1]
    half_rows = diag_inverse.shape[1]
    first_rhs = block_rhs[0]
    last_rhs = block_rhs[1]

    def solve_block(inverse, local_rhs):
        return product(inverse, lax.all_gather(local_rhs, "wide", axis=0, tiled=True))

    last_block = solve_block(diag_inverse[1], last_rhs)
    first_block = solve_block(diag_inverse[0], first_rhs - product(coupling, last_block))
    stacked = jnp.concatenate([first_block, last_block], axis=0)
    matching = lax.dynamic_slice_in_dim(stacked, narrow_index * panel_width, panel_width, 0)
    partial_value = product(upper_panel, matching)
    correction = lax.psum_scatter(partial_value, "narrow", scatter_dimension=1, tiled=True)
    solved_cols = lax.dynamic_slice_in_dim(stacked, narrow_index * own_targets, own_targets, 1)
    updated = upper_rhs - correction
    first_own = lax.dynamic_slice_in_dim(
        solved_cols[:half_rows], wide_index * block_rows, block_rows, 0
    )
    last_own = lax.dynamic_slice_in_dim(
        solved_cols[half_rows:], wide_index * block_rows, block_rows, 0
    )
    solved = jnp.stack([first_own, last_own])
    return (solved, updated)


def solution(mesh):
    return jax.shard_map(
        local,
        mesh=mesh,
        in_specs=(
            P("wide", "narrow"),
            P("wide", None),
            P(),
            P(None, "wide", None),
            P("wide", "narrow"),
        ),
        out_specs=(P(None, "wide", "narrow"), P("wide", "narrow")),
        check_vma=False,
    )
```

profile of v0, /device:TPU:1, one launch (start us, length us, event | category | flops | bytes accessed | tf_op | source)
XLA Modules:
  0.0 235.7 jit_solution(2569916423738369529)
XLA Ops:
  7.2 0.0 copy-start
  7.2 0.0 all-gather.6.cloned.1.call-start
  7.2 1.5 slice.20
  8.8 0.0 all-gather.6.cloned.1.call-update
  8.8 0.0 copy-start.6
  8.8 0.0 copy-start.7
  8.8 0.0 all-gather.4.cloned.1.call-start
  8.9 85.9 %all-gather.6.cloned.1.call-done = f32[1,512,2048]{2,1,0:T(8,128)} async-done(((f32[1,8,2048]{2,1,0:T(8,128)}), f32[1,512,2048]{2,1,0:T(8,128)}) %all-gather.6.cloned.1.call-update) | async-done | bytes 4194320 | tf_op jit(solution)/shard_map/all_gather | solution.py:22
  94.8 9.1 %fusion = f32[512,2048]{1,0:T(8,128)S(1)} fusion(f32[1,512,2048]{2,1,0:T(8,128)} %all-gather.6.cloned.1.call-done, f32[2,512,512]{2,1,0:T(8,128)} %param.7), kind=kOutput, calls=%fused_computation.4 | convolution fusion | flops 6442450944 | bytes 9437184 | tf_op jit(solution)/shard_map/dot_general | solution.py:8
  103.9 0.0 copy-start.1
  103.9 2.0 copy-done.1
  105.8 0.0 copy-done.6
  105.8 0.0 copy-done.7
  105.8 0.0 copy-start.4
  105.8 2.9 %fusion.2 = f32[8,2048]{1,0:T(8,128)} fusion(f32[512,2048]{1,0:T(8,128)S(1)} %fusion, f32[8,512]{1,0:T(8,128)S(1)} %copy-done.7, f32[2,8,2048]{2,1,0:T(8,128)S(1)} %copy-done.6), kind=kOutput, calls=%fused_computation.9 | convolution fusion | flops 100679680 | bytes 4341760 | tf_op jit(solution)/shard_map/dot_general | solution.py:8
  108.8 0.0 all-gather.4.cloned.1.call-update
  108.8 0.0 reduce-scatter.2.cloned.1.call-start
  108.8 76.3 %all-gather.4.cloned.1.call-done = f32[512,2048]{1,0:T(8,128)} async-done(((f32[8,2048]{1,0:T(8,128)}), f32[512,2048]{1,0:T(8,128)}) %all-gather.4.cloned.1.call-update) | async-done | bytes 4194320 | tf_op jit(solution)/shard_map/all_gather | solution.py:22
  185.1 0.0 copy-done.4
  185.1 0.0 copy-start.2
  185.1 8.8 %convolution_bitcast_fusion = f32[512,2048]{1,0:T(8,128)S(1)} fusion(f32[512,2048]{1,0:T(8,128)} %all-gather.4.cloned.1.call-done, f32[2,512,512]{2,1,0:T(8,128)S(1)} %copy-done.4), kind=kOutput, calls=%fused_computation.6 | convolution fusion | flops 6442450944 | bytes 9437184 | tf_op jit(solution)/shard_map/dot_general | solution.py:8
  194.0 0.0 copy-start.3
  194.0 2.0 copy-done.3
  196.0 0.0 copy-done
  196.0 0.0 copy-done.2
  196.0 3.5 %convolution_bitcast_fusion.1 = f32[240,2048]{1,0:T(8,128)} fusion(f32[240,256]{1,0:T(8,128)S(1)} %copy-done, s32[]{:T(128)S(6)} %select_n.12, f32[512,2048]{1,0:T(8,128)S(1)} %convolution_bitcast_fusion, f32[512,2048]{1,0:T(8,128)S(1)} %copy-done.2), kind=kOutput, calls=%fused_computation.7 | convolution fusion | flops 1510473728 | bytes 10600452 | tf_op jit(solution)/shard_map/dot_general | solution.py:8
  199.5 0.0 reduce-scatter.2.cloned.1.call-update
  199.5 1.7 fusion.5
  201.2 0.0 copy-start.5
  201.2 0.2 fusion.12
  201.4 0.6 pad_maximum_fusion
  202.1 25.3 %reduce-scatter.2.cloned.1.call-done = f32[240,512]{1,0:T(8,128)} async-done(((f32[240,2048]{1,0:T(8,128)}), f32[240,512]{1,0:T(8,128)}) %reduce-scatter.2.cloned.1.call-update) | async-done | bytes 491536 | tf_op jit(solution)/shard_map/reduce_scatter | solution.py:29
  227.3 0.0 copy-done.5
  227.3 1.9 sub.7
  (1 shorter events, 0.0 us)
Async XLA Ops:
  7.2 188.8 %copy-start = (f32[240,256]{1,0:T(8,128)S(1)}, f32[240,256]{1,0:T(8,128)}, u32[]{:S(2)}) copy-start(f32[240,256]{1,0:T(8,128)} %param.5) | copy-start | bytes 737284
  7.2 87.6 %all-gather.6.cloned.1.call-start = ((), (), s32[]{:S(2)}) async-start(), calls=%async_computation.3 | async-start | bytes 4259840 | tf_op jit(solution)/shard_map/all_gather | solution.py:22
  8.8 97.0 %copy-start.6 = (f32[2,8,2048]{2,1,0:T(8,128)S(1)}, f32[2,8,2048]{2,1,0:T(8,128)}, u32[]{:S(2)}) copy-start(f32[2,8,2048]{2,1,0:T(8,128)} %param.8) | copy-start | bytes 393220
  8.8 97.0 %copy-start.7 = (f32[8,512]{1,0:T(8,128)S(1)}, f32[8,512]{1,0:T(8,128)}, u32[]{:S(2)}) copy-start(f32[8,512]{1,0:T(8,128)} %param.6) | copy-start | bytes 49156
  8.8 176.3 %all-gather.4.cloned.1.call-start = ((), (), s32[]{:S(2)}) async-start(), calls=%async_computation.1 | async-start | bytes 4259840 | tf_op jit(solution)/shard_map/all_gather | solution.py:22
  103.9 2.0 copy-start.1
  105.8 79.3 %copy-start.4 = (f32[2,512,512]{2,1,0:T(8,128)S(1)}, f32[2,512,512]{2,1,0:T(8,128)}, u32[]{:S(2)}) copy-start(f32[2,512,512]{2,1,0:T(8,128)} %param.7) | copy-start | bytes 6291460
  108.8 118.6 %reduce-scatter.2.cloned.1.call-start = ((), (), s32[]{:S(2)}) async-start(), calls=%async_computation.2 | async-start | bytes 2457600 | tf_op jit(solution)/shard_map/reduce_scatter | solution.py:29
  185.1 10.8 %copy-start.2 = (f32[512,2048]{1,0:T(8,128)S(1)}, f32[512,2048]{1,0:T(8,128)}, u32[]{:S(2)}) copy-start(f32[512,2048]{1,0:T(8,128)} %copy-done.1) | copy-start | bytes 12582916
  194.0 2.0 copy-start.3
  201.2 26.1 %copy-start.5 = (f32[240,512]{1,0:T(8,128)S(1)}, f32[240,512]{1,0:T(8,128)}, u32[]{:S(2)}) copy-start(f32[240,512]{1,0:T(8,128)} %param.9) | copy-start | bytes 1474564
Sparse Core Ops, SparseCore 0:
  11.3 83.4 all-gather.5
  108.9 76.1 all-gather.3
  199.6 27.6 reduce-scatter.1
where the time goes:
time: 236 us
  waiting for transfers between devices  188 us (80%)
  matrix products  24.3 us (10%)
  between operations  13.8 us (6%)
  local copies, waits for them, and re-layouts  5.69 us (2%)
  other arithmetic  4.22 us (2%)
    all_gather x2, waiting for transfers between devices, solve_block(): lax.all_gather(local_rhs, 'wide', axis=0, tiled=True)  162 us
    reduce_scatter x1, waiting for transfers between devices, local(): lax.psum_scatter(partial_value, 'narrow', scatter_dimension=1, tiled=True)  25.3 us
    dot_general x4, matrix products, product(): jnp.dot(left, right, precision=lax.Precision.HIGHEST, preferred_element_t...  24.3 us
  transfers between devices with their start and end apart: 3, of which 3 were waited for; matrix products, arithmetic and copies ran while one was open for 1% of the time, Pallas kernels for 0%

commit v1 on v0

--- a/solution.py
+++ b/solution.py
@@ -19,7 +19,12 @@
     last_rhs = block_rhs[1]
 
     def solve_block(inverse, local_rhs):
-        return product(inverse, lax.all_gather(local_rhs, "wide", axis=0, tiled=True))
+        return product(
+            inverse,
+            jnp.concatenate(
+                lax.all_to_all(jnp.stack([local_rhs] * lax.axis_size("wide")), "wide", 0, 0), axis=0
+            ),
+        )
 
     last_block = solve_block(diag_inverse[1], last_rhs)
     first_block = solve_block(diag_inverse[0], first_rhs - product(coupling, last_block))

time: 236 us -> 285 us (1.21)
  blocking collectives: 0 us -> 109 us
  waiting for transfers between devices: 188 us -> 121 us
  starting transfers between devices: 0.12 us -> 6.24 us
    all_gather x2 -> x0, waiting for transfers between devices: 162 us -> none  [solve_block(): lax.all_gather(local_rhs, 'wide', axis=0, tiled=True)]
    all_to_all x0 -> x1, blocking collectives: none -> 109 us  [solve_block(): lax.all_to_all(jnp.stack([local_rhs] * lax.axis_size('wide')), 'wide', 0, 0)]
    all_to_all x0 -> x1, waiting for transfers between devices: none -> 95.6 us  [solve_block(): lax.all_to_all(jnp.stack([local_rhs] * lax.axis_size('wide')), 'wide', 0, 0)]
    all_to_all x0 -> x1, starting transfers between devices: none -> 6.02 us  [solve_block(): lax.all_to_all(jnp.stack([local_rhs] * lax.axis_size('wide')), 'wide', 0, 0)]
    another operation x0 -> x2, local copies, waits for them, and re-layouts: none -> 2.96 us  [solve_block(): jnp.stack([local_rhs] * lax.axis_size('wide'))]
  transfers between devices with their start and end apart: 3 -> 2, of which waited for: 3 -> 2; matrix products, arithmetic and copies ran while one was open for 1% -> 1% of each run, Pallas kernels for 0% -> 0%
where the time goes in v1:
time: 285 us; the launch traced here: 284 us
  waiting for transfers between devices  121 us (42%)
  blocking collectives  109 us (38%)
  matrix products  21.7 us (8%)
  between operations  14.1 us (5%)
  local copies, waits for them, and re-layouts  7.97 us (3%)
  starting transfers between devices  6.24 us (2%)
  other arithmetic  4.22 us (1%)
    all_to_all x1, blocking collectives, solve_block(): lax.all_to_all(jnp.stack([local_rhs] * lax.axis_size('wide')), 'wide', 0, 0)  109 us
    all_to_all x1, waiting for transfers between devices, solve_block(): lax.all_to_all(jnp.stack([local_rhs] * lax.axis_size('wide')), 'wide', 0, 0)  95.6 us
    reduce_scatter x1, waiting for transfers between devices, local(): lax.psum_scatter(partial_value, 'narrow', scatter_dimension=1, tiled=True)  25.1 us
    dot_general x4, matrix products, product(): jnp.dot(left, right, precision=lax.Precision.HIGHEST, preferred_element_t...  21.7 us
    all_to_all x1, starting transfers between devices, solve_block(): lax.all_to_all(jnp.stack([local_rhs] * lax.axis_size('wide')), 'wide', 0, 0)  6.02 us
  transfers between devices with their start and end apart: 2, of which 2 were waited for; matrix products, arithmetic and copies ran while one was open for 1% of the time, Pallas kernels for 0%

profile of v1, /device:TPU:1, one launch (start us, length us, event | category | flops | bytes accessed | tf_op | source)
XLA Modules:
  0.0 284.2 jit_solution(7767497454436882229)
XLA Ops:
  7.2 0.0 copy-start
  7.2 0.9 slice_bitcast_fusion
  8.1 0.5 stack.10
  8.6 0.0 copy-start.4
  8.6 109.2 %all_to_all.10 = f32[64,8,2048]{2,1,0:T(8,128)S(1)} all-to-all(f32[64,8,2048]{2,1,0:T(8,128)S(1)} %stack.10), channel_id=1, replica_groups=mesh['wide'=64,'narrow'=4] {'wide'}, dimensions={0} | all-to-all | bytes 8388608 | tf_op jit(solution)/shard_map/all_to_all | solution.py:25
  117.8 0.0 copy-done.4
  117.8 0.0 copy-start.6
  117.8 0.0 copy-start.7
  117.8 7.1 %fusion.2 = f32[512,2048]{1,0:T(8,128)S(1)} fusion(f32[64,8,2048]{2,1,0:T(8,128)S(1)} %all_to_all.10, f32[2,512,512]{2,1,0:T(8,128)S(1)} %copy-done.4), kind=kOutput, calls=%fused_computation.6 | convolution fusion | flops 6442450944 | bytes 9437184 | tf_op jit(solution)/shard_map/dot_general | solution.py:8
  124.9 0.0 copy-start.1
  124.9 1.9 copy-done.1
  126.9 0.0 copy-done.6
  126.9 0.0 copy-done.7
  126.9 2.3 fusion.7
  129.2 2.5 stack.11
  131.6 6.0 %all-to-all-start.1 = ((f32[64,8,2048]{2,1,0:T(8,128)}), f32[64,8,2048]{2,1,0:T(8,128)}, u32[]{:S(2)}, u32[]{:S(2)}) async-start(f32[64,8,2048]{2,1,0:T(8,128)} %stack.11), calls=%async_computation.1 | async-start | bytes 8388608 | tf_op jit(solution)/shard_map/all_to_all | solution.py:25
  137.7 0.2 reduce-scatter.2.cloned.1.call-start
  137.9 95.6 %all-to-all-done.1 = f32[64,8,2048]{2,1,0:T(8,128)} async-done(((f32[64,8,2048]{2,1,0:T(8,128)}), f32[64,8,2048]{2,1,0:T(8,128)}, u32[]{:S(2)}, u32[]{:S(2)}) %all-to-all-start.1) | async-done | bytes 4194336 | tf_op jit(solution)/shard_map/all_to_all | solution.py:25
  233.5 0.0 copy-start.2
  233.5 8.8 %fusion.4 = f32[512,2048]{1,0:T(8,128)S(1)} fusion(f32[64,8,2048]{2,1,0:T(8,128)} %all-to-all-done.1, f32[2,512,512]{2,1,0:T(8,128)S(1)} %copy-done.4), kind=kOutput, calls=%fused_computation.8 | convolution fusion | flops 6442450944 | bytes 9437184 | tf_op jit(solution)/shard_map/dot_general | solution.py:8
  242.4 0.0 copy-start.3
  242.4 2.0 copy-done.3
  244.3 0.0 copy-done
  244.3 0.0 copy-done.2
  244.3 3.5 %convolution_bitcast_fusion = f32[240,2048]{1,0:T(8,128)} fusion(f32[240,256]{1,0:T(8,128)S(1)} %copy-done, s32[]{:T(128)S(6)} %select_n.12, f32[512,2048]{1,0:T(8,128)S(1)} %fusion.4, f32[512,2048]{1,0:T(8,128)S(1)} %copy-done.2), kind=kOutput, calls=%fused_computation.9 | convolution fusion | flops 1510473728 | bytes 10600452 | tf_op jit(solution)/shard_map/dot_general | solution.py:8
  247.8 0.0 reduce-scatter.2.cloned.1.call-update
  247.8 1.7 fusion.10
  249.6 0.0 copy-start.5
  249.6 0.2 fusion.17
  249.8 0.6 pad_maximum_fusion
  250.4 25.1 %reduce-scatter.2.cloned.1.call-done = f32[240,512]{1,0:T(8,128)} async-done(((f32[240,2048]{1,0:T(8,128)}), f32[240,512]{1,0:T(8,128)}) %reduce-scatter.2.cloned.1.call-update) | async-done | bytes 491536 | tf_op jit(solution)/shard_map/reduce_scatter | solution.py:34
  275.5 0.0 copy-done.5
  275.5 1.9 sub.7
  (1 shorter events, 0.0 us)
Async XLA Ops:
  7.2 237.2 %copy-start = (f32[240,256]{1,0:T(8,128)S(1)}, f32[240,256]{1,0:T(8,128)}, u32[]{:S(2)}) copy-start(f32[240,256]{1,0:T(8,128)} %param.5) | copy-start | bytes 737284
  8.6 109.2 %copy-start.4 = (f32[2,512,512]{2,1,0:T(8,128)S(1)}, f32[2,512,512]{2,1,0:T(8,128)}, u32[]{:S(2)}) copy-start(f32[2,512,512]{2,1,0:T(8,128)} %param.7) | copy-start | bytes 6291460
  117.8 9.1 %copy-start.6 = (f32[2,8,2048]{2,1,0:T(8,128)S(1)}, f32[2,8,2048]{2,1,0:T(8,128)}, u32[]{:S(2)}) copy-start(f32[2,8,2048]{2,1,0:T(8,128)} %param.8) | copy-start | bytes 393220
  117.8 9.1 %copy-start.7 = (f32[8,512]{1,0:T(8,128)S(1)}, f32[8,512]{1,0:T(8,128)}, u32[]{:S(2)}) copy-start(f32[8,512]{1,0:T(8,128)} %param.6) | copy-start | bytes 49156
  124.9 2.0 copy-start.1
  131.6 101.9 %all-to-all-start.1 = ((f32[64,8,2048]{2,1,0:T(8,128)}), f32[64,8,2048]{2,1,0:T(8,128)}, u32[]{:S(2)}, u32[]{:S(2)}) async-start(f32[64,8,2048]{2,1,0:T(8,128)} %stack.11), calls=%async_computation.1 | async-start | bytes 8388608 | tf_op jit(solution)/shard_map/all_to_all | solution.py:25
  137.7 137.8 %reduce-scatter.2.cloned.1.call-start = ((), (), s32[]{:S(2)}) async-start(), calls=%async_computation.3 | async-start | bytes 2457600 | tf_op jit(solution)/shard_map/reduce_scatter | solution.py:34
  233.5 10.8 %copy-start.2 = (f32[512,2048]{1,0:T(8,128)S(1)}, f32[512,2048]{1,0:T(8,128)}, u32[]{:S(2)}) copy-start(f32[512,2048]{1,0:T(8,128)} %copy-done.1) | copy-start | bytes 12582916
  242.4 2.0 copy-start.3
  249.6 25.9 %copy-start.5 = (f32[240,512]{1,0:T(8,128)S(1)}, f32[240,512]{1,0:T(8,128)}, u32[]{:S(2)}) copy-start(f32[240,512]{1,0:T(8,128)} %param.9) | copy-start | bytes 1474564
Sparse Core Ops, SparseCore 0:
  247.9 27.5 reduce-scatter.1
